TPU v7x, 32 devices: a whole 2x2x4 slice. The times are simulated.
32 devices in a mesh: seq: 8 (over y, x, core), mp: 4 (over z).
Axes of the slice: x: 2, y: 2, z: 4, core: 2. Of those that a mesh axis runs over, the one named last changes fastest.
Arguments:
- coarse: bfloat16 [768, 1024], P('mp', 'seq'), may hold values from -6 to 6
- skip: bfloat16 [768, 2048], P('mp', 'seq'), may hold values from -6 to 6
- conv_weight: bfloat16 [3, 768, 768], P(None, 'mp'), may hold values from -0.125 to 0.125
- conv_bias: float32 [768], P('mp'), may hold values from -3 to 3
- head_weight: bfloat16 [768, 512], P(None, 'mp'), may hold values from -0.21875 to 0.21875
- head_bias: float32 [512], P('mp'), may hold values from -3 to 3
- counts: int32 [2048, 512], P('seq', 'mp'), may hold values from 0 to 3
- seg_mask: int32 [1, 512], P(None, 'mp'), may hold values 0 or 1
Outputs:
- grad_skip: bfloat16 [768, 2048], P('mp', 'seq')
- grad_coarse: bfloat16 [768, 1024], P('mp', 'seq')
- grad_head: float32 [768, 512], P('seq', 'mp')
- grad_conv: float32 [768, 3, 768], P('seq', None, 'mp')
All inputs are finite; a program needn't handle non-finite values. No bound on the sum of `seg_mask` on one device may be relied on, other than what follows from the above.
Results may differ from a plain program's by a relative error of at most 0.0068.
Values may be sent and summed in bfloat16 or wider, within the bound.
No kernel may reach another device: no remote copies, remote signals or barrier semaphores. Data moves between devices by JAX's collectives and lax.ppermute only.
A program may use at most 64 MiB of HBM per device.

v0:
```python
import math
import jax
import jax.numpy as jnp
from jax import lax
from jax.sharding import PartitionSpec as P

root_two_pi = 0.7978845608028654
cubic_coef = 0.044715
multi_weight = 5.0
pseudo_count = 0.5


def extended(block, sides, width):
    for axis, dim in sides:
        count = lax.axis_size(axis)
        forward = [(i, i + 1) for i in range(count - 1)]
        backward = [(target, source) for source, target in forward]
        low = lax.ppermute(
            lax.slice_in_dim(block, block.shape[dim] - width, None, axis=dim), axis, forward
        )
        high = lax.ppermute(lax.slice_in_dim(block, 0, width, axis=dim), axis, backward)
        block = jnp.concatenate([low, block, high], axis=dim)
    return block


def gelu_value(inputs):
    inner = root_two_pi * (inputs + cubic_coef * inputs * inputs * inputs)
    return 0.5 * inputs * (1.0 + jnp.tanh(inner))


def gelu_slope(inputs):
    inner = root_two_pi * (inputs + cubic_coef * inputs * inputs * inputs)
    tangent = jnp.tanh(inner)
    return 0.5 * (1.0 + tangent) + 0.5 * inputs * (1.0 - tangent * tangent) * root_two_pi * (
        1.0 + 3.0 * cubic_coef * inputs * inputs
    )


def contract_first(left, right):
    return lax.dot_general(
        left, right, (((0,), (0,)), ((), ())), preferred_element_type=jnp.float32
    )


def contract_last(left, right):
    return lax.dot_general(
        left, right, (((1,), (1,)), ((), ())), preferred_element_type=jnp.float32
    )


def shards(coarse, skip, conv_weight, conv_bias, head_weight, head_bias, counts, seg_mask):
    width_dev = skip.shape[0]
    length_dev = skip.shape[1]
    taps = conv_weight.shape[0]
    reach = taps // 2
    seq_count = lax.axis_size("seq")
    scale_back = 1.0 / math.sqrt(length_dev * seq_count)
    doubled = jnp.repeat(coarse.astype(jnp.float32), 2, axis=1)
    summed = (doubled + skip.astype(jnp.float32)).astype(jnp.bfloat16)
    padded = extended(summed, (("seq", 1),), reach)
    widened = lax.all_gather(padded, "mp", axis=0, tiled=True)
    conv_out = jnp.zeros((width_dev, length_dev), jnp.float32)
    for offset in range(taps):
        conv_out = conv_out + jnp.dot(
            conv_weight[offset],
            widened[:, offset : offset + length_dev],
            preferred_element_type=jnp.float32,
        )
    before = conv_out + conv_bias[:, None]
    hidden = (summed.astype(jnp.float32) + gelu_value(before)).astype(jnp.bfloat16)
    hidden_full = lax.all_gather(hidden, "mp", axis=0, tiled=True)
    logits = contract_first(hidden_full, head_weight) + head_bias
    predicted = jax.nn.softplus(logits) + pseudo_count
    observed = counts.astype(jnp.float32)
    pred_sum = jnp.sum(predicted, axis=0)
    count_sum = jnp.sum(observed, axis=0)
    span = min(8, seq_count)
    position = lax.axis_index("seq")
    segment = position // span
    seg_count = seq_count // span
    member = (jnp.arange(seg_count, dtype=jnp.int32) == segment).astype(jnp.float32)[:, None]
    pred_table, count_table = lax.psum(
        (member * pred_sum[None, :], member * count_sum[None, :]), "seq"
    )
    pred_total = jnp.sum(member * pred_table, axis=0)
    count_total = jnp.sum(member * count_table, axis=0)
    mask_row = lax.dynamic_slice_in_dim(seg_mask, segment, 1, 0).astype(jnp.float32)
    slope_pred = mask_row * (
        1.0 + (multi_weight - 1.0) * count_total / pred_total - multi_weight * observed / predicted
    )
    grad_logits = (slope_pred * jax.nn.sigmoid(logits)).astype(jnp.bfloat16)
    track_full = lax.all_gather(grad_logits, "mp", axis=1, tiled=True)
    head_own = lax.all_to_all(head_weight, "mp", split_axis=0, concat_axis=1, tiled=True)
    grad_hidden = contract_last(head_own, track_full)
    grad_head = (
        lax.psum_scatter(
            jnp.dot(hidden_full, grad_logits, preferred_element_type=jnp.float32),
            "seq",
            scatter_dimension=0,
            tiled=True,
        )
        * scale_back
    )
    grad_before = (grad_hidden * gelu_slope(before)).astype(jnp.bfloat16)
    grad_padded = extended(grad_before, (("seq", 1),), reach)
    weight_rows = lax.all_to_all(conv_weight, "mp", split_axis=2, concat_axis=1, tiled=True)
    carry = jnp.zeros((width_dev, length_dev), jnp.float32)
    piece = lax.all_gather(grad_padded, "mp", axis=0, tiled=True)
    for offset in range(taps):
        first_row = 2 * reach - offset
        block = weight_rows[offset]
        carry = carry + contract_first(block, piece[:, first_row : first_row + length_dev])
    grad_input = grad_hidden + carry
    grad_skip = grad_input.astype(jnp.bfloat16)
    grad_coarse = jnp.sum(grad_input.reshape(width_dev, length_dev // 2, 2), axis=2).astype(
        jnp.bfloat16
    )
    grad_conv = (
        lax.psum_scatter(
            jnp.stack(
                [
                    contract_last(widened[:, offset : offset + length_dev], grad_before)
                    for offset in range(taps)
                ],
                axis=1,
            ),
            "seq",
            scatter_dimension=0,
            tiled=True,
        )
        * scale_back
    )
    return (grad_skip, grad_coarse, grad_head, grad_conv)


def solution(mesh):
    in_specs = (
        P("mp", "seq"),
        P("mp", "seq"),
        P(None, "mp", None),
        P("mp"),
        P(None, "mp"),
        P("mp"),
        P("seq", "mp"),
        P(None, "mp"),
    )
    out_specs = (P("mp", "seq"), P("mp", "seq"), P("seq", "mp"), P("seq", None, "mp"))
    return jax.shard_map(shards, mesh=mesh, in_specs=in_specs, out_specs=out_specs, check_vma=False)
```

profile of v0, /device:TPU:0, one launch (start us, length us, event | category | flops | bytes accessed | tf_op | source)
XLA Modules:
  0.0 156.0 jit_solution(14249767625792272399)
XLA Ops:
  7.2 0.9 copy.29
  8.2 0.2 reshape.54
  8.5 0.9 add_convert_fusion.1
  9.5 1.3 collective-permute-start.1
  10.8 3.0 %collective-permute-start = (bf16[192,1]{1,0:T(8,128)(2,1)S(1)}, bf16[192,1]{1,0:T(8,128)(2,1)S(1)}, u32[]{:S(2)}, u32[]{:S(2)}) collective-permute-start(bf16[192,1]{1,0:T(8,128)(2,1)S(1)} %get-tuple-element.27), channel_id=1, source_target_pairs={{0,4},{4,8},{8,12},{12,16},{16,20},{20,24},{24,28},{1,5},{5,9},{9,... | collective-permute-start | bytes 1160 | tf_op jit(solution)/shard_map/ppermute | solution.py:18
  13.9 6.4 %all-to-all-start = ((bf16[4,192,128]{2,1,0:T(8,128)(2,1)}), bf16[4,192,128]{2,1,0:T(8,128)(2,1)S(1)}, u32[]{:S(2)}, u32[]{:S(2)}) async-start(bf16[4,192,128]{2,1,0:T(8,128)(2,1)} %bitcast.9), calls=%async_computation | async-start | bytes 393216 | tf_op jit(solution)/shard_map/all_to_all | solution.py:93
  20.3 0.1 maximum_bitcast_fusion
  20.6 18.7 %all-gather = bf16[4,192,258]{1,2,0:T(8,128)(2,1)S(1)} all-gather(bf16[1,192,258]{1,2,0:T(8,128)(2,1)S(1)} %copy.31), channel_id=1, replica_groups=mesh['seq'=8,'mp'=4] {'mp'}, dimensions={0}, use_global_device_ids=true | all-gather | bytes 495360 | tf_op jit(solution)/shard_map/all_gather | solution.py:61
  39.3 0.2 copy.32
  39.6 0.5 reshape.57
  40.1 0.3 fusion.13
  40.4 0.3 convolution_add_fusion.3
  40.7 0.4 add_convert_fusion
  41.1 15.0 %all_gather.13 = bf16[768,256]{1,0:T(8,128)(2,1)S(1)} all-gather(bf16[192,256]{1,0:T(8,128)(2,1)S(1)} %get-tuple-element.29), channel_id=1, replica_groups=mesh['seq'=8,'mp'=4] {'mp'}, dimensions={0}, use_global_device_ids=true | all-gather | bytes 491520 | tf_op jit(solution)/shard_map/all_gather | solution.py:71
  56.2 1.3 fusion.31
  57.5 11.8 %all-reduce = (f32[1,128]{1,0:T(1,128)S(1)}, f32[1,128]{1,0:T(1,128)S(1)}) all-reduce(f32[1,128]{1,0:T(1,128)S(1)} %get-tuple-element.37, f32[1,128]{1,0:T(1,128)S(1)} %get-tuple-element.38), channel_id=1, replica_groups=mesh['seq'=8,'mp'=4] {'seq'}, use_global_device_ids=true, to_apply=%region_3.4 | all-reduce | flops 256 | bytes 2048 | tf_op jit(solution)/shard_map/psum | solution.py:82
  69.3 0.1 multiply_convert_fusion
  69.4 1.0 fusion.36
  70.5 13.3 %all_gather.14 = bf16[256,512]{1,0:T(8,128)(2,1)S(1)} all-gather(bf16[256,128]{1,0:T(8,128)(2,1)S(1)} %multiply_convert_fusion), channel_id=1, replica_groups=mesh['seq'=8,'mp'=4] {'mp'}, dimensions={1}, use_global_device_ids=true | all-gather | bytes 327680 | tf_op jit(solution)/shard_map/all_gather | solution.py:92
  83.9 0.3 fusion.27
  84.2 0.2 convolution_bitcast_fusion.2
  84.4 0.3 convolution_bitcast_fusion.1
  84.7 0.3 convolution_bitcast_fusion
  85.1 1.8 %copy.43 = f32[768,576]{1,0:T(8,128)} copy(f32[768,576]{0,1:T(8,128)S(1)} %bitcast.80) | data formatting | bytes 3538944
  86.9 2.2 %copy.36 = bf16[3,192,768]{1,0,2:T(4,128)(2,1)} copy(bf16[3,192,768]{2,1,0:T(8,128)(2,1)S(1)} %copy-done) | data formatting | bytes 1769472 | tf_op args[2]
  89.1 3.6 %all-to-all-start.1 = ((bf16[3,192,768]{1,0,2:T(4,128)(2,1)}), bf16[3,192,768]{1,0,2:T(4,128)(2,1)S(1)}, u32[]{:S(2)}, u32[]{:S(2)}) async-start(bf16[3,192,768]{1,0,2:T(4,128)(2,1)} %copy.36), calls=%async_computation.1 | async-start | bytes 3145728 | tf_op jit(solution)/shard_map/all_to_all | solution.py:106
  92.7 1.3 collective-permute-start.3
  94.0 3.0 %collective-permute-start.2 = (bf16[192,1]{1,0:T(8,128)(2,1)S(1)}, bf16[192,1]{1,0:T(8,128)(2,1)S(1)}, u32[]{:S(2)}, u32[]{:S(2)}) collective-permute-start(bf16[192,1]{1,0:T(8,128)(2,1)S(1)} %get-tuple-element.25), channel_id=1, source_target_pairs={{0,4},{4,8},{8,12},{12,16},{16,20},{20,24},{24,28},{1,5},{5,9},{9,... | collective-permute-start | bytes 1160 | tf_op jit(solution)/shard_map/ppermute | solution.py:18
  97.1 0.9 collective-permute-done.2
  98.2 39.4 %all-gather.1 = bf16[4,192,258]{1,2,0:T(8,128)(2,1)S(1)} all-gather(bf16[1,192,258]{1,2,0:T(8,128)(2,1)S(1)} %copy.34), channel_id=1, replica_groups=mesh['seq'=8,'mp'=4] {'mp'}, dimensions={0}, use_global_device_ids=true | all-gather | bytes 495360 | tf_op jit(solution)/shard_map/all_gather | solution.py:108
  137.6 0.2 copy.35
  137.8 0.5 reshape.59
  138.4 1.4 broadcast_multiply_fusion.1
  139.8 1.1 copy.53
  140.9 0.4 fusion.32
  141.3 0.3 squeeze.21
  141.7 0.3 squeeze.22
  142.0 0.3 squeeze.23
  142.4 0.3 fusion.6
  142.7 0.3 convolution_add_fusion.1
  143.0 0.9 fusion.35
  144.0 0.1 copy.38
  144.1 0.1 reshape.55
  144.2 0.3 reduce_sum.29
  144.6 0.7 copy.39
  145.3 1.8 %reduce-scatter.7.cloned.1.call-done = f32[96,576]{1,0:T(8,128)} async-done(((f32[768,576]{1,0:T(8,128)}), f32[96,576]{1,0:T(8,128)}) %reduce-scatter.7.cloned.1.call-update) | async-done | bytes 221200
  147.2 1.1 copy.44
  148.3 0.9 copy.40
  (33 shorter events, 1.1 us)
Async XLA Ops:
  7.2 13.1 %copy-start.1 = (s32[256,128]{1,0:T(8,128)S(1)}, s32[256,128]{1,0:T(8,128)}, u32[]{:S(2)}) copy-start(s32[256,128]{1,0:T(8,128)} %param.14) | copy-start | bytes 393220
  7.2 13.1 %copy-start.3 = (s32[1,128]{1,0:T(1,128)S(1)}, s32[1,128]{1,0:T(1,128)}, u32[]{:S(2)}) copy-start(s32[1,128]{1,0:T(1,128)} %param.15) | copy-start | bytes 1540
  9.5 10.8 %collective-permute-start.1 = (bf16[192,1]{1,0:T(8,128)(2,1)S(1)}, bf16[192,1]{1,0:T(8,128)(2,1)S(1)}, u32[]{:S(2)}, u32[]{:S(2)}) collective-permute-start(bf16[192,1]{1,0:T(8,128)(2,1)S(1)} %get-tuple-element.28), channel_id=1, source_target_pairs={{4,0},{8,4},{12,8},{16,12},{20,16},{24,20},{28,24},{5,1},{9,5},{13... | collective-permute-start | bytes 1160 | tf_op jit(solution)/shard_map/ppermute | solution.py:21
  10.8 9.5 %collective-permute-start = (bf16[192,1]{1,0:T(8,128)(2,1)S(1)}, bf16[192,1]{1,0:T(8,128)(2,1)S(1)}, u32[]{:S(2)}, u32[]{:S(2)}) collective-permute-start(bf16[192,1]{1,0:T(8,128)(2,1)S(1)} %get-tuple-element.27), channel_id=1, source_target_pairs={{0,4},{4,8},{8,12},{12,16},{16,20},{20,24},{24,28},{1,5},{5,9},{9,... | collective-permute-start | bytes 1160 | tf_op jit(solution)/shard_map/ppermute | solution.py:18
  13.9 70.0 %all-to-all-start = ((bf16[4,192,128]{2,1,0:T(8,128)(2,1)}), bf16[4,192,128]{2,1,0:T(8,128)(2,1)S(1)}, u32[]{:S(2)}, u32[]{:S(2)}) async-start(bf16[4,192,128]{2,1,0:T(8,128)(2,1)} %bitcast.9), calls=%async_computation | async-start | bytes 393216 | tf_op jit(solution)/shard_map/all_to_all | solution.py:93
  20.2 19.9 %copy-start = (bf16[3,192,768]{2,1,0:T(8,128)(2,1)S(1)}, bf16[3,192,768]{2,1,0:T(8,128)(2,1)}, u32[]{:S(2)}) copy-start(bf16[3,192,768]{2,1,0:T(8,128)(2,1)} %param.10) | copy-start | bytes 2654212
  20.2 118.1 %reduce-scatter.5.cloned.1.call-start = ((), (), s32[]{:S(2)}) async-start(), calls=%async_computation.4 | async-start | bytes 442368 | tf_op jit(solution)/shard_map/reduce_scatter | solution.py:96
  39.5 1.2 copy-start.2
  40.4 15.7 %copy-start.4 = (f32[128]{0:T(128)S(1)}, f32[128]{0:T(128)}, u32[]{:S(2)}) copy-start(f32[128]{0:T(128)} %param.13) | copy-start | bytes 1540
  70.5 76.7 %reduce-scatter.7.cloned.1.call-start = ((), (), s32[]{:S(2)}) async-start(), calls=%async_computation.5 | async-start | bytes 2211840
  89.1 50.7 %all-to-all-start.1 = ((bf16[3,192,768]{1,0,2:T(4,128)(2,1)}), bf16[3,192,768]{1,0,2:T(4,128)(2,1)S(1)}, u32[]{:S(2)}, u32[]{:S(2)}) async-start(bf16[3,192,768]{1,0,2:T(4,128)(2,1)} %copy.36), calls=%async_computation.1 | async-start | bytes 3145728 | tf_op jit(solution)/shard_map/all_to_all | solution.py:106
  92.7 4.3 %collective-permute-start.3 = (bf16[192,1]{1,0:T(8,128)(2,1)S(1)}, bf16[192,1]{1,0:T(8,128)(2,1)S(1)}, u32[]{:S(2)}, u32[]{:S(2)}) collective-permute-start(bf16[192,1]{1,0:T(8,128)(2,1)S(1)} %get-tuple-element.26), channel_id=1, source_target_pairs={{4,0},{8,4},{12,8},{16,12},{20,16},{24,20},{28,24},{5,1},{9,5},{13... | collective-permute-start | bytes 1160 | tf_op jit(solution)/shard_map/ppermute | solution.py:21
  94.0 3.9 %collective-permute-start.2 = (bf16[192,1]{1,0:T(8,128)(2,1)S(1)}, bf16[192,1]{1,0:T(8,128)(2,1)S(1)}, u32[]{:S(2)}, u32[]{:S(2)}) collective-permute-start(bf16[192,1]{1,0:T(8,128)(2,1)S(1)} %get-tuple-element.25), channel_id=1, source_target_pairs={{0,4},{4,8},{8,12},{12,16},{16,20},{20,24},{24,28},{1,5},{5,9},{9,... | collective-permute-start | bytes 1160 | tf_op jit(solution)/shard_map/ppermute | solution.py:18
Sparse Core Ops, SparseCore 0:
  70.6 32.9 reduce-scatter.4
  107.0 40.1 reduce-scatter.6
where the time goes:
time: 157 us; the launch traced here: 156 us
  blocking collectives  98.3 us (63%)
  starting transfers between devices  18.6 us (12%)
  between operations  14.4 us (9%)
  local copies, waits for them, and re-layouts  12.7 us (8%)
  matrix products  5.91 us (4%)
  other arithmetic  3.27 us (2%)
  waiting for transfers between devices  2.76 us (2%)
    all_gather x1, blocking collectives, shards(): piece = lax.all_gather(grad_padded, 'mp', axis=0, tiled=True)  39.4 us
    all_gather x1, blocking collectives, shards(): widened = lax.all_gather(padded, 'mp', axis=0, tiled=True)  18.7 us
    all_gather x1, blocking collectives, shards(): hidden_full = lax.all_gather(hidden, 'mp', axis=0, tiled=True)  15 us
    all_gather x1, blocking collectives, shards(): track_full = lax.all_gather(grad_logits, 'mp', axis=1, tiled=True)  13.3 us
    psum x1, blocking collectives, shards(): lax.psum((member * pred_sum[None, :], member * count_sum[None, :]), 'seq')  11.8 us
    unnamed x19, local copies, waits for them, and re-layouts  8 us
    all_to_all x1, starting transfers between devices, shards(): lax.all_to_all(head_weight, 'mp', split_axis=0, concat_axis=1, tiled=True)  6.36 us
    ppermute x2, starting transfers between devices, extended(): lax.ppermute(lax.slice_in_dim(block, block.shape[dim] - width, None, axis...  6.07 us
  transfers between devices with their start and end apart: 8, of which 2 were waited for; matrix products, arithmetic and copies ran while one was open for 11% of the time, Pallas kernels for 0%

commit v1 on v0

--- a/solution.py
+++ b/solution.py
@@ -89,7 +89,7 @@
         1.0 + (multi_weight - 1.0) * count_total / pred_total - multi_weight * observed / predicted
     )
     grad_logits = (slope_pred * jax.nn.sigmoid(logits)).astype(jnp.bfloat16)
-    track_full = lax.all_gather(grad_logits, "mp", axis=1, tiled=True)
+    track_full = jnp.concatenate(lax.all_gather(grad_logits, "mp"), 1)
     head_own = lax.all_to_all(head_weight, "mp", split_axis=0, concat_axis=1, tiled=True)
     grad_hidden = contract_last(head_own, track_full)
     grad_head = (

time: 157 us -> 157 us (level)
  no operation moved by 1% of the time
where the time goes in v1:
time: 157 us; the launch traced here: 156 us
  blocking collectives  98.6 us (63%)
  starting transfers between devices  18.6 us (12%)
  between operations  14.4 us (9%)
  local copies, waits for them, and re-layouts  12.7 us (8%)
  matrix products  5.91 us (4%)
  other arithmetic  3.27 us (2%)
  waiting for transfers between devices  2.46 us (2%)
    all_gather x1, blocking collectives, shards(): piece = lax.all_gather(grad_padded, 'mp', axis=0, tiled=True)  38.8 us
    all_gather x1, blocking collectives, shards(): widened = lax.all_gather(padded, 'mp', axis=0, tiled=True)  18.7 us
    all_gather x1, blocking collectives, shards(): hidden_full = lax.all_gather(hidden, 'mp', axis=0, tiled=True)  15 us
    all_gather x1, blocking collectives, shards(): track_full = jnp.concatenate(lax.all_gather(grad_logits, 'mp'), 1)  14.3 us
    psum x1, blocking collectives, shards(): lax.psum((member * pred_sum[None, :], member * count_sum[None, :]), 'seq')  11.8 us
    unnamed x19, local copies, waits for them, and re-layouts  8 us
    all_to_all x1, starting transfers between devices, shards(): lax.all_to_all(head_weight, 'mp', split_axis=0, concat_axis=1, tiled=True)  6.36 us
    ppermute x2, starting transfers between devices, extended(): lax.ppermute(lax.slice_in_dim(block, block.shape[dim] - width, None, axis...  6.07 us
  transfers between devices with their start and end apart: 8, of which 2 were waited for; matrix products, arithmetic and copies ran while one was open for 11% of the time, Pallas kernels for 0%

profile of v1, /device:TPU:0, one launch (start us, length us, event | category | flops | bytes accessed | tf_op | source)
XLA Modules:
  0.0 156.0 jit_solution(9052603000118449284)
XLA Ops:
  7.2 0.9 copy.27
  8.2 0.2 reshape.58
  8.5 0.9 add_convert_fusion.1
  9.5 1.3 collective-permute-start.1
  10.8 3.0 %collective-permute-start = (bf16[192,1]{1,0:T(8,128)(2,1)S(1)}, bf16[192,1]{1,0:T(8,128)(2,1)S(1)}, u32[]{:S(2)}, u32[]{:S(2)}) collective-permute-start(bf16[192,1]{1,0:T(8,128)(2,1)S(1)} %get-tuple-element.27), channel_id=1, source_target_pairs={{0,4},{4,8},{8,12},{12,16},{16,20},{20,24},{24,28},{1,5},{5,9},{9,... | collective-permute-start | bytes 1160 | tf_op jit(solution)/shard_map/ppermute | solution.py:18
  13.9 6.4 %all-to-all-start = ((bf16[4,192,128]{2,1,0:T(8,128)(2,1)}), bf16[4,192,128]{2,1,0:T(8,128)(2,1)S(1)}, u32[]{:S(2)}, u32[]{:S(2)}) async-start(bf16[4,192,128]{2,1,0:T(8,128)(2,1)} %bitcast.11), calls=%async_computation | async-start | bytes 393216 | tf_op jit(solution)/shard_map/all_to_all | solution.py:93
  20.3 0.1 maximum_bitcast_fusion
  20.6 18.7 %all-gather.1 = bf16[4,192,258]{1,2,0:T(8,128)(2,1)S(1)} all-gather(bf16[1,192,258]{1,2,0:T(8,128)(2,1)S(1)} %copy.29), channel_id=1, replica_groups=mesh['seq'=8,'mp'=4] {'mp'}, dimensions={0}, use_global_device_ids=true | all-gather | bytes 495360 | tf_op jit(solution)/shard_map/all_gather | solution.py:61
  39.3 0.2 copy.30
  39.6 0.5 reshape.63
  40.1 0.3 fusion.13
  40.4 0.3 convolution_add_fusion.3
  40.7 0.4 add_convert_fusion
  41.1 15.0 %all_gather.16 = bf16[768,256]{1,0:T(8,128)(2,1)S(1)} all-gather(bf16[192,256]{1,0:T(8,128)(2,1)S(1)} %get-tuple-element.29), channel_id=1, replica_groups=mesh['seq'=8,'mp'=4] {'mp'}, dimensions={0}, use_global_device_ids=true | all-gather | bytes 491520 | tf_op jit(solution)/shard_map/all_gather | solution.py:71
  56.2 1.3 fusion.30
  57.5 11.8 %all-reduce = (f32[1,128]{1,0:T(1,128)S(1)}, f32[1,128]{1,0:T(1,128)S(1)}) all-reduce(f32[1,128]{1,0:T(1,128)S(1)} %get-tuple-element.37, f32[1,128]{1,0:T(1,128)S(1)} %get-tuple-element.38), channel_id=1, replica_groups=mesh['seq'=8,'mp'=4] {'seq'}, use_global_device_ids=true, to_apply=%region_3.4 | all-reduce | flops 256 | bytes 2048 | tf_op jit(solution)/shard_map/psum | solution.py:82
  69.3 0.1 multiply_convert_fusion
  69.4 1.0 fusion.35
  70.5 14.3 %all-gather = bf16[1024,128]{1,0:T(8,128)(2,1)S(1)} all-gather(bf16[256,128]{1,0:T(8,128)(2,1)S(1)} %multiply_convert_fusion), channel_id=2, replica_groups=mesh['seq'=8,'mp'=4] {'mp'}, dimensions={0}, use_global_device_ids=true | all-gather | bytes 327680 | tf_op jit(solution)/shard_map/all_gather | solution.py:92
  84.8 0.3 fusion.27
  85.1 0.2 convolution_bitcast_fusion.2
  85.3 0.3 convolution_bitcast_fusion.1
  85.6 0.3 convolution_bitcast_fusion
  86.0 1.8 %copy.40 = f32[768,576]{1,0:T(8,128)} copy(f32[768,576]{0,1:T(8,128)S(1)} %bitcast.80) | data formatting | bytes 3538944
  87.9 2.2 %copy.33 = bf16[3,192,768]{1,0,2:T(4,128)(2,1)} copy(bf16[3,192,768]{2,1,0:T(8,128)(2,1)S(1)} %copy-done) | data formatting | bytes 1769472 | tf_op args[2]
  90.0 3.6 %all-to-all-start.1 = ((bf16[3,192,768]{1,0,2:T(4,128)(2,1)}), bf16[3,192,768]{1,0,2:T(4,128)(2,1)S(1)}, u32[]{:S(2)}, u32[]{:S(2)}) async-start(bf16[3,192,768]{1,0,2:T(4,128)(2,1)} %copy.33), calls=%async_computation.1 | async-start | bytes 3145728 | tf_op jit(solution)/shard_map/all_to_all | solution.py:106
  93.7 1.3 collective-permute-start.3
  95.0 3.0 %collective-permute-start.2 = (bf16[192,1]{1,0:T(8,128)(2,1)S(1)}, bf16[192,1]{1,0:T(8,128)(2,1)S(1)}, u32[]{:S(2)}, u32[]{:S(2)}) collective-permute-start(bf16[192,1]{1,0:T(8,128)(2,1)S(1)} %get-tuple-element.25), channel_id=1, source_target_pairs={{0,4},{4,8},{8,12},{12,16},{16,20},{20,24},{24,28},{1,5},{5,9},{9,... | collective-permute-start | bytes 1160 | tf_op jit(solution)/shard_map/ppermute | solution.py:18
  98.0 0.9 collective-permute-done.2
  99.1 38.8 %all-gather.2 = bf16[4,192,258]{1,2,0:T(8,128)(2,1)S(1)} all-gather(bf16[1,192,258]{1,2,0:T(8,128)(2,1)S(1)} %copy.31), channel_id=1, replica_groups=mesh['seq'=8,'mp'=4] {'mp'}, dimensions={0}, use_global_device_ids=true | all-gather | bytes 495360 | tf_op jit(solution)/shard_map/all_gather | solution.py:108
  137.9 0.2 copy.32
  138.1 0.5 reshape.65
  138.7 1.4 broadcast_multiply_fusion.1
  140.1 1.1 copy.43
  141.2 0.4 fusion.31
  141.6 0.3 squeeze.21
  142.0 0.3 squeeze.22
  142.3 0.3 squeeze.23
  142.7 0.3 fusion.6
  143.0 0.3 convolution_add_fusion.1
  143.3 0.9 fusion.34
  144.3 0.1 copy.35
  144.4 0.1 reshape.60
  144.6 0.3 reduce_sum.29
  144.9 0.7 copy.36
  145.6 1.5 reduce-scatter.7.cloned.1.call-done
  147.2 1.1 copy.41
  148.3 0.9 copy.37
  (33 shorter events, 1.1 us)
Async XLA Ops:
  7.2 13.1 %copy-start.1 = (s32[256,128]{1,0:T(8,128)S(1)}, s32[256,128]{1,0:T(8,128)}, u32[]{:S(2)}) copy-start(s32[256,128]{1,0:T(8,128)} %param.14) | copy-start | bytes 393220
  7.2 13.1 %copy-start.3 = (s32[1,128]{1,0:T(1,128)S(1)}, s32[1,128]{1,0:T(1,128)}, u32[]{:S(2)}) copy-start(s32[1,128]{1,0:T(1,128)} %param.15) | copy-start | bytes 1540
  9.5 10.8 %collective-permute-start.1 = (bf16[192,1]{1,0:T(8,128)(2,1)S(1)}, bf16[192,1]{1,0:T(8,128)(2,1)S(1)}, u32[]{:S(2)}, u32[]{:S(2)}) collective-permute-start(bf16[192,1]{1,0:T(8,128)(2,1)S(1)} %get-tuple-element.28), channel_id=1, source_target_pairs={{4,0},{8,4},{12,8},{16,12},{20,16},{24,20},{28,24},{5,1},{9,5},{13... | collective-permute-start | bytes 1160 | tf_op jit(solution)/shard_map/ppermute | solution.py:21
  10.8 9.5 %collective-permute-start = (bf16[192,1]{1,0:T(8,128)(2,1)S(1)}, bf16[192,1]{1,0:T(8,128)(2,1)S(1)}, u32[]{:S(2)}, u32[]{:S(2)}) collective-permute-start(bf16[192,1]{1,0:T(8,128)(2,1)S(1)} %get-tuple-element.27), channel_id=1, source_target_pairs={{0,4},{4,8},{8,12},{12,16},{16,20},{20,24},{24,28},{1,5},{5,9},{9,... | collective-permute-start | bytes 1160 | tf_op jit(solution)/shard_map/ppermute | solution.py:18
  13.9 70.9 %all-to-all-start = ((bf16[4,192,128]{2,1,0:T(8,128)(2,1)}), bf16[4,192,128]{2,1,0:T(8,128)(2,1)S(1)}, u32[]{:S(2)}, u32[]{:S(2)}) async-start(bf16[4,192,128]{2,1,0:T(8,128)(2,1)} %bitcast.11), calls=%async_computation | async-start | bytes 393216 | tf_op jit(solution)/shard_map/all_to_all | solution.py:93
  20.2 19.9 %copy-start = (bf16[3,192,768]{2,1,0:T(8,128)(2,1)S(1)}, bf16[3,192,768]{2,1,0:T(8,128)(2,1)}, u32[]{:S(2)}) copy-start(bf16[3,192,768]{2,1,0:T(8,128)(2,1)} %param.10) | copy-start | bytes 2654212
  20.2 118.4 %reduce-scatter.5.cloned.1.call-start = ((), (), s32[]{:S(2)}) async-start(), calls=%async_computation.4 | async-start | bytes 442368 | tf_op jit(solution)/shard_map/reduce_scatter | solution.py:96
  39.5 1.2 copy-start.2
  40.4 15.7 %copy-start.4 = (f32[128]{0:T(128)S(1)}, f32[128]{0:T(128)}, u32[]{:S(2)}) copy-start(f32[128]{0:T(128)} %param.13) | copy-start | bytes 1540
  70.5 76.7 %reduce-scatter.7.cloned.1.call-start = ((), (), s32[]{:S(2)}) async-start(), calls=%async_computation.5 | async-start | bytes 2211840
  90.0 50.1 %all-to-all-start.1 = ((bf16[3,192,768]{1,0,2:T(4,128)(2,1)}), bf16[3,192,768]{1,0,2:T(4,128)(2,1)S(1)}, u32[]{:S(2)}, u32[]{:S(2)}) async-start(bf16[3,192,768]{1,0,2:T(4,128)(2,1)} %copy.33), calls=%async_computation.1 | async-start | bytes 3145728 | tf_op jit(solution)/shard_map/all_to_all | solution.py:106
  93.7 4.3 %collective-permute-start.3 = (bf16[192,1]{1,0:T(8,128)(2,1)S(1)}, bf16[192,1]{1,0:T(8,128)(2,1)S(1)}, u32[]{:S(2)}, u32[]{:S(2)}) collective-permute-start(bf16[192,1]{1,0:T(8,128)(2,1)S(1)} %get-tuple-element.26), channel_id=1, source_target_pairs={{4,0},{8,4},{12,8},{16,12},{20,16},{24,20},{28,24},{5,1},{9,5},{13... | collective-permute-start | bytes 1160 | tf_op jit(solution)/shard_map/ppermute | solution.py:21
  95.0 3.9 %collective-permute-start.2 = (bf16[192,1]{1,0:T(8,128)(2,1)S(1)}, bf16[192,1]{1,0:T(8,128)(2,1)S(1)}, u32[]{:S(2)}, u32[]{:S(2)}) collective-permute-start(bf16[192,1]{1,0:T(8,128)(2,1)S(1)} %get-tuple-element.25), channel_id=1, source_target_pairs={{0,4},{4,8},{8,12},{12,16},{16,20},{20,24},{24,28},{1,5},{5,9},{9,... | collective-permute-start | bytes 1160 | tf_op jit(solution)/shard_map/ppermute | solution.py:18
Sparse Core Ops, SparseCore 0:
  70.6 32.9 reduce-scatter.4
  107.0 40.0 reduce-scatter.6
